TPU v7x, 32 devices: a whole 2x2x4 slice. The times are simulated.
32 devices in a mesh: replica: 8 (over z, core), shard: 4 (over y, x).
Axes of the slice: x: 2, y: 2, z: 4, core: 2. Of those that a mesh axis runs over, the one named last changes fastest.
Arguments:
- local_weights: bfloat16 [8, 8192, 512], P('replica', 'shard'), may hold values from -1.3258252 to 1.3258252
- outer_base: bfloat16 [8192, 512], P('shard'), may hold values from -0.0625 to 0.0625
- momentum: bfloat16 [8192, 512], P('shard', 'replica'), may hold values from -0.06591797 to 0.06591797
- error_feedback: bfloat16 [8, 8192, 512], P('replica', 'shard'), may hold values from -0.032958984 to 0.032958984
- q_start: float32 [512, 32], replicated, may hold values from -6 to 6
- tokens: bfloat16 [8, 512, 8192], P('replica', None, 'shard'), may hold values from -6 to 6
Outputs:
- new_base: bfloat16 [8192, 512], P('shard')
- new_momentum: bfloat16 [8192, 512], P('shard', 'replica')
- new_error: bfloat16 [8, 8192, 512], P('replica', 'shard')
- key_rows: bfloat16 [8, 512, 512], P('replica', 'shard')
All inputs are finite; a program needn't handle non-finite values.
Results may differ from a plain program's by a relative error of at most 0.0065.
Values may be sent and summed in bfloat16 or wider, within the bound.
A program may use at most 64 MiB of HBM per device.

v0:
```python
import jax
import jax.numpy as jnp
from jax import lax
from jax.sharding import PartitionSpec as P

outer_mu = 0.9
outer_rate = 0.7


def on_device(local_weights, outer_base, momentum, error_feedback, q_start, tokens):
    highest = lax.Precision.HIGHEST
    replicas = lax.axis_size("replica")
    own_columns = momentum.shape[1]
    full_momentum = lax.all_gather(momentum, "replica", axis=1, tiled=True)
    pseudo = (
        outer_base.astype(jnp.float32)
        - local_weights[0].astype(jnp.float32)
        + error_feedback[0].astype(jnp.float32)
    )
    p_local = jnp.dot(pseudo, q_start, precision=highest)
    p_mean = lax.psum(p_local, "replica") / replicas
    own_gram = jnp.dot(p_mean.T, p_mean, precision=highest)
    gram_sum = lax.psum(own_gram, "shard")
    factor_low = jnp.linalg.cholesky(gram_sum)
    basis = jax.scipy.linalg.solve_triangular(factor_low, p_mean.T, lower=True).T
    q_raw = jnp.dot(pseudo.T, basis, precision=highest)
    q_mean = lax.psum(q_raw, ("replica", "shard")) / replicas
    update = jnp.dot(basis, q_mean.T, precision=highest)
    new_error = (pseudo - update).astype(jnp.bfloat16)[None]
    moment = outer_mu * full_momentum.astype(jnp.float32) + update
    new_base = (outer_base.astype(jnp.float32) - outer_rate * (outer_mu * moment + update)).astype(
        jnp.bfloat16
    )
    first_column = lax.axis_index("replica") * own_columns
    new_momentum = lax.dynamic_slice_in_dim(moment, first_column, own_columns, 1).astype(
        jnp.bfloat16
    )
    own_tokens = tokens[0]
    key_sum = lax.psum_scatter(
        jnp.dot(own_tokens, new_base, preferred_element_type=jnp.float32),
        "shard",
        scatter_dimension=0,
        tiled=True,
    )
    key_rows = key_sum.astype(jnp.bfloat16)[None]
    return (new_base, new_momentum, new_error, key_rows)


def solution(mesh):
    in_specs = (
        P("replica", "shard", None),
        P("shard", None),
        P("shard", "replica"),
        P("replica", "shard", None),
        P(),
        P("replica", None, "shard"),
    )
    out_specs = (
        P("shard", None),
        P("shard", "replica"),
        P("replica", "shard", None),
        P("replica", "shard", None),
    )
    return jax.shard_map(
        on_device, mesh=mesh, in_specs=in_specs, out_specs=out_specs, check_vma=False
    )
```

profile of v0, /device:TPU:0, one launch (start us, length us, event | category | flops | bytes accessed | tf_op | source)
XLA Modules:
  0.0 319.2 jit_solution(3947755793024692435)
XLA Ops:
  7.2 0.0 copy-start
  7.2 0.0 all-reduce.3.cloned.1.call-start
  7.2 4.1 %copy.10 = bf16[2048,512]{0,1:T(8,128)(2,1)} copy(bf16[2048,512]{1,0:T(8,128)(2,1)} %param.7) | data formatting | bytes 4194304 | tf_op args[1]
  11.3 4.0 %copy.11 = bf16[1,2048,512]{1,2,0:T(8,128)(2,1)} copy(bf16[1,2048,512]{2,1,0:T(8,128)(2,1)} %param.6) | data formatting | bytes 4194304 | tf_op args[0]
  15.3 0.0 copy-start.6
  15.3 3.9 %copy.12 = bf16[1,2048,512]{1,2,0:T(8,128)(2,1)} copy(bf16[1,2048,512]{2,1,0:T(8,128)(2,1)} %param.9) | data formatting | bytes 4194304 | tf_op args[3]
  19.2 0.0 copy-done.6
  19.2 6.8 %fusion.10 = f32[2048,32]{0,1:T(8,128)} fusion(f32[512,32]{0,1:T(8,128)S(1)} %copy-done.6, bf16[2048,512]{0,1:T(8,128)(2,1)} %copy.10, bf16[1,2048,512]{1,2,0:T(8,128)(2,1)} %copy.12, bf16[1,2048,512]{1,2,0:T(8,128)(2,1)} %copy.11), kind=kOutput, calls=%fused_computation.11 | convolution fusion | flops 407896064 | bytes 6619136 | tf_op jit(solution)/shard_map/dot_general | solution.py:20
  26.0 0.0 all-reduce.3.cloned.1.call-update
  26.0 0.0 all-reduce.5.cloned.1.call-start
  26.1 58.3 %all-reduce.3.cloned.1.call-done = f32[2048,32]{0,1:T(8,128)} async-done(((f32[2048,32]{0,1:T(8,128)}), f32[2048,32]{0,1:T(8,128)}) %all-reduce.3.cloned.1.call-update) | async-done | bytes 262160 | tf_op jit(solution)/shard_map/psum | solution.py:21
  84.3 1.4 fusion.16
  85.7 16.0 %psum.22 = f32[32,32]{0,1:T(8,128)S(1)} all-reduce(f32[32,32]{0,1:T(8,128)S(1)} %fusion.16), channel_id=1, replica_groups=mesh['replica'=8,'shard'=4] {'shard'}, use_global_device_ids=true, to_apply=%region_1.0 | all-reduce | flops 1024 | bytes 8192 | tf_op jit(solution)/shard_map/psum | solution.py:23
  101.7 0.1 copy.14
  101.8 2.9 cholesky.16
  104.7 0.6 compare_reduce_fusion
  105.4 0.7 fusion.21
  106.0 2.4 custom-call.7
  108.4 1.4 fusion.14
  109.8 6.4 %fusion.8 = f32[512,32]{1,0:T(8,128)} fusion(f32[32,2048]{1,0:T(8,128)S(1)} %fusion.14, bf16[2048,512]{0,1:T(8,128)(2,1)} %copy.10, bf16[1,2048,512]{1,2,0:T(8,128)(2,1)} %copy.12, bf16[1,2048,512]{1,2,0:T(8,128)(2,1)} %copy.11), kind=kOutput, calls=%fused_computation.10 | convolution fusion | flops 407896064 | bytes 6619136 | tf_op jit(solution)/shard_map/dot_general | solution.py:26
  116.2 0.0 all-reduce.5.cloned.1.call-update
  116.3 0.0 all-gather.2.cloned.1.call-start
  116.3 0.7 all-gather.2.cloned.1.call-update
  117.0 0.2 reduce-scatter.2.cloned.1.call-start
  117.2 123.0 %all-reduce.5.cloned.1.call-done = f32[512,32]{1,0:T(8,128)} async-done(((f32[512,32]{1,0:T(8,128)}), f32[512,32]{1,0:T(8,128)}) %all-reduce.5.cloned.1.call-update) | async-done | bytes 65552 | tf_op jit(solution)/shard_map/psum | solution.py:27
  240.2 29.8 %all-gather.2.cloned.1.call-done = bf16[2048,512]{0,1:T(8,128)(2,1)} async-done(((bf16[2048,64]{0,1:T(8,128)(2,1)}), bf16[2048,512]{0,1:T(8,128)(2,1)}) %all-gather.2.cloned.1.call-update) | async-done | bytes 2097168 | tf_op jit(solution)/shard_map/all_gather | solution.py:14
  270.1 0.0 copy-start.1
  270.1 0.0 copy-start.2
  270.1 0.0 copy-start.3
  270.1 0.0 copy-start.4
  270.1 6.3 %multiply_add_fusion = (bf16[2048,512]{0,1:T(8,128)(2,1)}, f32[2048,512]{0,1:T(8,128)S(1)}) fusion(bf16[2048,512]{0,1:T(8,128)(2,1)} %all-gather.2.cloned.1.call-done, f32[32,2048]{1,0:T(8,128)S(1)} %fusion.14, f32[512,32]{1,0:T(8,128)} %all-reduce.5.cloned.1.call-done), kind=kOutput, calls=%fused_computation.5 | convolution fusion | flops 406863872 | bytes 8716288 | tf_op jit(solution)/shard_map/dot_general | solution.py:28
  276.4 0.0 copy-done.1
  276.4 0.0 copy-done.2
  276.4 0.0 copy-done.3
  276.4 0.0 copy-done.4
  276.4 3.5 %fusion.2 = (bf16[1,2048,512]{1,2,0:T(8,128)(2,1)}, bf16[2048,512]{0,1:T(8,128)(2,1)S(1)}) fusion(f32[2048,512]{0,1:T(8,128)S(1)} %get-tuple-element.11, bf16[1,2048,512]{1,2,0:T(8,128)(2,1)S(1)} %copy-done.3, bf16[1,2048,512]{1,2,0:T(8,128)(2,1)S(1)} %copy-done.2, bf16[2048,512]{0,1:T(8,128)(2,1)S(1)} %copy-done.1, bf16[2048,512]{0,1:T(8,128)(2,1)S(1)} %copy-done.4), kind=kLoop, calls=%fused_computation.6 | loop fusion | flops 15728640 | bytes 16777216 | tf_op jit(solution)/shard_map/broadcast_in_dim | solution.py:29
  279.8 0.0 copy-start.5
  279.9 1.3 copy-done.5
  281.2 0.0 copy-done
  281.2 2.3 fusion.5
  283.4 0.0 reduce-scatter.2.cloned.1.call-update
  283.5 3.9 %copy.15 = bf16[2048,512]{1,0:T(8,128)(2,1)} copy(bf16[2048,512]{0,1:T(8,128)(2,1)} %copy-done.5) | data formatting | bytes 4194304
  287.4 4.0 %copy.16 = bf16[1,2048,512]{2,1,0:T(8,128)(2,1)} copy(bf16[1,2048,512]{1,2,0:T(8,128)(2,1)} %get-tuple-element.8) | data formatting | bytes 4194304
  291.3 1.7 dynamic-slice_convert_fusion
  293.0 17.9 %reduce-scatter.2.cloned.1.call-done = f32[128,512]{0,1:T(8,128)} async-done(((f32[512,512]{0,1:T(8,128)}), f32[128,512]{0,1:T(8,128)}) %reduce-scatter.2.cloned.1.call-update) | async-done | bytes 262160 | tf_op jit(solution)/shard_map/reduce_scatter | solution.py:39
  310.9 1.0 convert_bitcast_fusion
  311.9 0.8 copy.17
  (2 shorter events, 0.0 us)
Async XLA Ops:
  7.2 274.0 %copy-start = (bf16[1,512,2048]{2,1,0:T(8,128)(2,1)S(1)}, bf16[1,512,2048]{2,1,0:T(8,128)(2,1)}, u32[]{:S(2)}) copy-start(bf16[1,512,2048]{2,1,0:T(8,128)(2,1)} %param.11) | copy-start | bytes 6291460
  7.2 77.1 %all-reduce.3.cloned.1.call-start = ((), (), s32[]{:S(2)}) async-start(), calls=%async_computation.2 | async-start | bytes 524288 | tf_op jit(solution)/shard_map/psum | solution.py:21
  15.3 3.9 %copy-start.6 = (f32[512,32]{0,1:T(8,128)S(1)}, f32[512,32]{0,1:T(8,128)}, u32[]{:S(2)}) copy-start(f32[512,32]{0,1:T(8,128)} %param.10) | copy-start | bytes 196612
  26.0 214.2 %all-reduce.5.cloned.1.call-start = ((), (), s32[]{:S(2)}) async-start(), calls=%async_computation.3 | async-start | bytes 524288 | tf_op jit(solution)/shard_map/psum | solution.py:27
  116.3 153.8 %all-gather.2.cloned.1.call-start = ((), (), s32[]{:S(2)}) async-start(), calls=%async_computation.1 | async-start | bytes 2359296 | tf_op jit(solution)/shard_map/all_gather | solution.py:14
  117.0 193.9 %reduce-scatter.2.cloned.1.call-start = ((), (), s32[]{:S(2)}) async-start(), calls=%async_computation.4 | async-start | bytes 1310720 | tf_op jit(solution)/shard_map/reduce_scatter | solution.py:39
  270.1 6.3 %copy-start.1 = (bf16[2048,512]{0,1:T(8,128)(2,1)S(1)}, bf16[2048,512]{0,1:T(8,128)(2,1)}, u32[]{:S(2)}) copy-start(bf16[2048,512]{0,1:T(8,128)(2,1)} %copy.10) | copy-start | bytes 6291460
  270.1 6.3 %copy-start.2 = (bf16[1,2048,512]{1,2,0:T(8,128)(2,1)S(1)}, bf16[1,2048,512]{1,2,0:T(8,128)(2,1)}, u32[]{:S(2)}) copy-start(bf16[1,2048,512]{1,2,0:T(8,128)(2,1)} %copy.11) | copy-start | bytes 6291460
  270.1 6.3 %copy-start.3 = (bf16[1,2048,512]{1,2,0:T(8,128)(2,1)S(1)}, bf16[1,2048,512]{1,2,0:T(8,128)(2,1)}, u32[]{:S(2)}) copy-start(bf16[1,2048,512]{1,2,0:T(8,128)(2,1)} %copy.12) | copy-start | bytes 6291460
  270.1 6.3 %copy-start.4 = (bf16[2048,512]{0,1:T(8,128)(2,1)S(1)}, bf16[2048,512]{0,1:T(8,128)(2,1)}, u32[]{:S(2)}) copy-start(bf16[2048,512]{0,1:T(8,128)(2,1)} %all-gather.2.cloned.1.call-done) | copy-start | bytes 6291460
  279.8 1.3 copy-start.5
Sparse Core Ops, SparseCore 0:
  26.1 58.1 all-reduce.2
  116.4 123.7 all-reduce.4
  241.8 28.1 all-gather.1
  283.6 27.3 reduce-scatter.1
where the time goes:
time: 320 us; the launch traced here: 319 us
  waiting for transfers between devices  230 us (72%)
  matrix products  24.5 us (8%)
  local copies, waits for them, and re-layouts  23.7 us (7%)
  blocking collectives  16 us (5%)
  between operations  13.8 us (4%)
  other arithmetic  11.1 us (3%)
    psum x1, waiting for transfers between devices, on_device(): q_mean = lax.psum(q_raw, ('replica', 'shard')) / replicas  123 us
    psum x1, waiting for transfers between devices, on_device(): p_mean = lax.psum(p_local, 'replica') / replicas  58.3 us
    all_gather x1, waiting for transfers between devices, on_device(): full_momentum = lax.all_gather(momentum, 'replica', axis=1, tiled=True)  29.8 us
    unnamed x20, local copies, waits for them, and re-layouts  22 us
    reduce_scatter x1, waiting for transfers between devices, on_device(): lax.psum_scatter(jnp.dot(own_tokens, new_base, preferred_element_type=jnp...  17.9 us
    psum x1, blocking collectives, on_device(): gram_sum = lax.psum(own_gram, 'shard')  16 us
    dot_general x1, matrix products, on_device(): p_local = jnp.dot(pseudo, q_start, precision=highest)  6.77 us
  transfers between devices with their start and end apart: 4, of which 4 were waited for; matrix products, arithmetic and copies ran while one was open for 3% of the time, Pallas kernels for 0%

commit v1 on v0

--- a/solution.py
+++ b/solution.py
@@ -5,6 +5,10 @@
 
 outer_mu = 0.9
 outer_rate = 0.7
+
+
+def move_bars(original):
+    return jax.lax.all_gather(original, "replica").sum(axis=0)
 
 
 def on_device(local_weights, outer_base, momentum, error_feedback, q_start, tokens):
@@ -18,7 +22,7 @@
         + error_feedback[0].astype(jnp.float32)
     )
     p_local = jnp.dot(pseudo, q_start, precision=highest)
-    p_mean = lax.psum(p_local, "replica") / replicas
+    p_mean = move_bars(p_local) / replicas
     own_gram = jnp.dot(p_mean.T, p_mean, precision=highest)
     gram_sum = lax.psum(own_gram, "shard")
     factor_low = jnp.linalg.cholesky(gram_sum)

time: 320 us -> 270 us (0.84)
  waiting for transfers between devices: 230 us -> 178 us
    psum x1 -> x0, waiting for transfers between devices: 58.3 us -> none  [on_device(): p_mean = lax.psum(p_local, 'replica') / replicas]
    all_gather x0 -> x1, waiting for transfers between devices: none -> 31.2 us  [move_bars(): return jax.lax.all_gather(original, 'replica').sum(axis=0)]
    all_gather x1, waiting for transfers between devices: 29.8 us -> 0.02 us  [on_device(): full_momentum = lax.all_gather(momentum, 'replica', axis=1, tiled=True)]
    psum x1, waiting for transfers between devices: 123 us -> 129 us  [on_device(): q_mean = lax.psum(q_raw, ('replica', 'shard')) / replicas]
    unnamed x20 -> x21, local copies, waits for them, and re-layouts: 22 us -> 24.8 us
  transfers between devices with their start and end apart: 4 -> 4, of which waited for: 4 -> 3; matrix products, arithmetic and copies ran while one was open for 3% -> 10% of each run, Pallas kernels for 0% -> 0%
where the time goes in v1:
time: 270 us; the launch traced here: 269 us
  waiting for transfers between devices  178 us (66%)
  local copies, waits for them, and re-layouts  26.5 us (10%)
  matrix products  22.5 us (8%)
  blocking collectives  16 us (6%)
  between operations  13.8 us (5%)
  other arithmetic  11.7 us (4%)
    psum x1, waiting for transfers between devices, on_device(): q_mean = lax.psum(q_raw, ('replica', 'shard')) / replicas  129 us
    all_gather x1, waiting for transfers between devices, move_bars(): return jax.lax.all_gather(original, 'replica').sum(axis=0)  31.2 us
    unnamed x21, local copies, waits for them, and re-layouts  24.8 us
    reduce_scatter x1, waiting for transfers between devices, on_device(): lax.psum_scatter(jnp.dot(own_tokens, new_base, preferred_element_type=jnp...  17.6 us
    psum x1, blocking collectives, on_device(): gram_sum = lax.psum(own_gram, 'shard')  16 us
    dot_general x1, matrix products, on_device(): p_local = jnp.dot(pseudo, q_start, precision=highest)  6.77 us
    dot_general x1, matrix products, on_device(): q_raw = jnp.dot(pseudo.T, basis, precision=highest)  6.42 us
    dot_general x1, matrix products, on_device(): update = jnp.dot(basis, q_mean.T, precision=highest)  6.28 us
  transfers between devices with their start and end apart: 4, of which 3 were waited for; matrix products, arithmetic and copies ran while one was open for 10% of the time, Pallas kernels for 0%

profile of v1, /device:TPU:0, one launch (start us, length us, event | category | flops | bytes accessed | tf_op | source)
XLA Modules:
  0.0 269.1 jit_solution(13298006584807507915)
XLA Ops:
  7.2 0.0 copy-start
  7.2 0.0 all-gather.6.cloned.1.call-start
  7.2 4.1 %copy.18 = bf16[2048,512]{0,1:T(8,128)(2,1)} copy(bf16[2048,512]{1,0:T(8,128)(2,1)} %param.7) | data formatting | bytes 4194304 | tf_op args[1]
  11.3 4.0 %copy.19 = bf16[1,2048,512]{1,2,0:T(8,128)(2,1)} copy(bf16[1,2048,512]{2,1,0:T(8,128)(2,1)} %param.6) | data formatting | bytes 4194304 | tf_op args[0]
  15.3 0.0 copy-start.6
  15.3 3.9 %copy.20 = bf16[1,2048,512]{1,2,0:T(8,128)(2,1)} copy(bf16[1,2048,512]{2,1,0:T(8,128)(2,1)} %param.9) | data formatting | bytes 4194304 | tf_op args[3]
  19.2 0.0 copy-done.6
  19.2 6.8 %fusion.10 = f32[2048,32]{0,1:T(8,128)} fusion(f32[512,32]{0,1:T(8,128)S(1)} %copy-done.6, bf16[2048,512]{0,1:T(8,128)(2,1)} %copy.18, bf16[1,2048,512]{1,2,0:T(8,128)(2,1)} %copy.20, bf16[1,2048,512]{1,2,0:T(8,128)(2,1)} %copy.19), kind=kOutput, calls=%fused_computation.12 | convolution fusion | flops 407896064 | bytes 6619136 | tf_op jit(solution)/shard_map/dot_general | solution.py:24
  26.0 0.0 all-gather.6.cloned.1.call-update
  26.0 0.0 all-gather.4.cloned.1.call-start
  26.1 0.7 all-gather.4.cloned.1.call-update
  26.8 0.0 all-reduce.2.cloned.1.call-start
  26.8 31.2 %all-gather.6.cloned.1.call-done = f32[16384,32]{0,1:T(8,128)} async-done(((f32[2048,32]{0,1:T(8,128)}), f32[16384,32]{0,1:T(8,128)}) %all-gather.6.cloned.1.call-update) | async-done | bytes 2097168 | tf_op jit(solution)/shard_map/all_gather | solution.py:11
  58.0 2.8 %copy.27 = f32[4,8,8,2048]{3,2,1,0:T(8,128)S(1)} copy(f32[4,8,8,2048]{3,1,2,0:T(8,128)} %bitcast.43) | data formatting | bytes 4194304
  60.8 0.5 bitcast_reduce_fusion
  61.4 0.4 fusion.16
  61.7 16.0 %psum.14 = f32[32,32]{0,1:T(8,128)S(1)} all-reduce(f32[32,32]{0,1:T(8,128)S(1)} %fusion.16), channel_id=1, replica_groups=mesh['replica'=8,'shard'=4] {'shard'}, use_global_device_ids=true, to_apply=%region_1.0 | all-reduce | flops 1024 | bytes 8192 | tf_op jit(solution)/shard_map/psum | solution.py:27
  77.7 0.1 copy.22
  77.8 2.9 %cholesky.16 = f32[32,32]{1,0:T(8,128)S(1)} custom-call(f32[32,32]{1,0:T(8,128)S(1)} %fusion.23), custom_call_target="Cholesky" | custom-call | tf_op jit(solution)/shard_map/jit(cholesky)/cholesky | solution.py:28
  80.8 0.6 compare_reduce_fusion
  81.4 0.7 fusion.21
  82.1 2.4 custom-call.7
  84.5 0.4 fusion.14
  84.9 6.4 %fusion.8 = f32[512,32]{1,0:T(8,128)} fusion(f32[32,2048]{1,0:T(8,128)S(1)} %fusion.14, bf16[2048,512]{0,1:T(8,128)(2,1)} %copy.18, bf16[1,2048,512]{1,2,0:T(8,128)(2,1)} %copy.20, bf16[1,2048,512]{1,2,0:T(8,128)(2,1)} %copy.19), kind=kOutput, calls=%fused_computation.11 | convolution fusion | flops 407896064 | bytes 6619136 | tf_op jit(solution)/shard_map/dot_general | solution.py:30
  91.4 0.0 all-reduce.2.cloned.1.call-update
  91.4 0.2 reduce-scatter.2.cloned.1.call-start
  91.6 0.0 all-gather.4.cloned.1.call-done
  91.6 128.7 %all-reduce.2.cloned.1.call-done = f32[512,32]{1,0:T(8,128)} async-done(((f32[512,32]{1,0:T(8,128)}), f32[512,32]{1,0:T(8,128)}) %all-reduce.2.cloned.1.call-update) | async-done | bytes 65552 | tf_op jit(solution)/shard_map/psum | solution.py:31
  220.3 0.0 copy-start.1
  220.3 0.0 copy-start.2
  220.3 0.0 copy-start.3
  220.3 0.0 copy-start.4
  220.3 6.3 %multiply_add_fusion = (bf16[2048,512]{0,1:T(8,128)(2,1)}, f32[2048,512]{0,1:T(8,128)S(1)}) fusion(bf16[2048,512]{0,1:T(8,128)(2,1)} %all-gather.4.cloned.1.call-done, f32[32,2048]{1,0:T(8,128)S(1)} %fusion.14, f32[512,32]{1,0:T(8,128)} %all-reduce.2.cloned.1.call-done), kind=kOutput, calls=%fused_computation.5 | convolution fusion | flops 406863872 | bytes 8716288 | tf_op jit(solution)/shard_map/dot_general | solution.py:32
  226.6 0.0 copy-done.1
  226.6 0.0 copy-done.2
  226.6 0.0 copy-done.3
  226.6 0.0 copy-done.4
  226.6 3.5 %fusion.2 = (bf16[1,2048,512]{1,2,0:T(8,128)(2,1)}, bf16[2048,512]{0,1:T(8,128)(2,1)S(1)}) fusion(f32[2048,512]{0,1:T(8,128)S(1)} %get-tuple-element.15, bf16[1,2048,512]{1,2,0:T(8,128)(2,1)S(1)} %copy-done.3, bf16[1,2048,512]{1,2,0:T(8,128)(2,1)S(1)} %copy-done.2, bf16[2048,512]{0,1:T(8,128)(2,1)S(1)} %copy-done.1, bf16[2048,512]{0,1:T(8,128)(2,1)S(1)} %copy-done.4), kind=kLoop, calls=%fused_computation.6 | loop fusion | flops 15728640 | bytes 16777216 | tf_op jit(solution)/shard_map/broadcast_in_dim | solution.py:33
  230.1 0.0 copy-start.5
  230.1 1.3 copy-done.5
  231.4 0.0 copy-done
  231.4 2.3 fusion.5
  233.7 0.0 reduce-scatter.2.cloned.1.call-update
  233.7 3.9 %copy.23 = bf16[2048,512]{1,0:T(8,128)(2,1)} copy(bf16[2048,512]{0,1:T(8,128)(2,1)} %copy-done.5) | data formatting | bytes 4194304
  237.6 3.9 %copy.24 = bf16[1,2048,512]{2,1,0:T(8,128)(2,1)} copy(bf16[1,2048,512]{1,2,0:T(8,128)(2,1)} %get-tuple-element.12) | data formatting | bytes 4194304
  241.5 1.7 dynamic-slice_convert_fusion
  243.2 17.6 %reduce-scatter.2.cloned.1.call-done = f32[128,512]{0,1:T(8,128)} async-done(((f32[512,512]{0,1:T(8,128)}), f32[128,512]{0,1:T(8,128)}) %reduce-scatter.2.cloned.1.call-update) | async-done | bytes 262160 | tf_op jit(solution)/shard_map/reduce_scatter | solution.py:43
  260.8 1.0 convert_bitcast_fusion
  261.8 0.8 copy.25
  (2 shorter events, 0.0 us)
Async XLA Ops:
  7.2 224.2 %copy-start = (bf16[1,512,2048]{2,1,0:T(8,128)(2,1)S(1)}, bf16[1,512,2048]{2,1,0:T(8,128)(2,1)}, u32[]{:S(2)}) copy-start(bf16[1,512,2048]{2,1,0:T(8,128)(2,1)} %param.11) | copy-start | bytes 6291460
  7.2 50.9 %all-gather.6.cloned.1.call-start = ((), (), s32[]{:S(2)}) async-start(), calls=%async_computation.4 | async-start | bytes 2359296 | tf_op jit(solution)/shard_map/all_gather | solution.py:11
  15.3 3.9 %copy-start.6 = (f32[512,32]{0,1:T(8,128)S(1)}, f32[512,32]{0,1:T(8,128)}, u32[]{:S(2)}) copy-start(f32[512,32]{0,1:T(8,128)} %param.10) | copy-start | bytes 196612
  26.0 65.6 %all-gather.4.cloned.1.call-start = ((), (), s32[]{:S(2)}) async-start(), calls=%async_computation.1 | async-start | bytes 2359296 | tf_op jit(solution)/shard_map/all_gather | solution.py:18
  26.8 193.5 %all-reduce.2.cloned.1.call-start = ((), (), s32[]{:S(2)}) async-start(), calls=%async_computation.2 | async-start | bytes 524288 | tf_op jit(solution)/shard_map/psum | solution.py:31
  91.4 169.4 %reduce-scatter.2.cloned.1.call-start = ((), (), s32[]{:S(2)}) async-start(), calls=%async_computation.3 | async-start | bytes 1310720 | tf_op jit(solution)/shard_map/reduce_scatter | solution.py:43
  220.3 6.3 %copy-start.1 = (bf16[2048,512]{0,1:T(8,128)(2,1)S(1)}, bf16[2048,512]{0,1:T(8,128)(2,1)}, u32[]{:S(2)}) copy-start(bf16[2048,512]{0,1:T(8,128)(2,1)} %copy.18) | copy-start | bytes 6291460
  220.3 6.3 %copy-start.2 = (bf16[1,2048,512]{1,2,0:T(8,128)(2,1)S(1)}, bf16[1,2048,512]{1,2,0:T(8,128)(2,1)}, u32[]{:S(2)}) copy-start(bf16[1,2048,512]{1,2,0:T(8,128)(2,1)} %copy.19) | copy-start | bytes 6291460
  220.3 6.3 %copy-start.3 = (bf16[1,2048,512]{1,2,0:T(8,128)(2,1)S(1)}, bf16[1,2048,512]{1,2,0:T(8,128)(2,1)}, u32[]{:S(2)}) copy-start(bf16[1,2048,512]{1,2,0:T(8,128)(2,1)} %copy.20) | copy-start | bytes 6291460
  220.3 6.3 %copy-start.4 = (bf16[2048,512]{0,1:T(8,128)(2,1)S(1)}, bf16[2048,512]{0,1:T(8,128)(2,1)}, u32[]{:S(2)}) copy-start(bf16[2048,512]{0,1:T(8,128)(2,1)} %all-gather.4.cloned.1.call-done) | copy-start | bytes 6291460
  230.1 1.3 copy-start.5
Sparse Core Ops, SparseCore 0:
  26.1 31.8 all-gather.5
  59.6 28.5 all-gather.3
  94.3 125.9 all-reduce.1
  233.8 26.9 reduce-scatter.1
